TPU v7x, 512 devices: a whole 4x8x8 slice. The times are simulated.
512 devices in a mesh: asset: 64 (over y, z), rhs: 8 (over x, core).
Axes of the slice: x: 4, y: 8, z: 8, core: 2. Of those that a mesh axis runs over, the one named last changes fastest.
Arguments:
- targets: float32 [65536, 1024], P('asset', 'rhs'), may hold values from -27 to 27
- ridge: float32 [65536], P('asset'), may hold values from 0.8 to 2.5
- blocks: bfloat16 [512, 16, 128, 128], P('asset', None, 'rhs'), may hold values from -0.046875 to 0.046875
- col_index: int32 [512, 16], P('asset'), may hold values from 0 to 511, as said below
- row_length: int32 [512], P('asset'), may hold values from 8 to 16, as said below
Outputs:
- solution: float32 [65536, 1024], P('asset', 'rhs')
- residual: float32 [65536, 1024], P('asset', 'rhs')
Inputs may be any that keep to these rules, and one draw needn't show every extreme that they name: `col_index`: the block columns of row i are distinct and lie within 8 blocks of i, counted cyclically modulo 512; slots at or past row_length[i] hold such columns too and are ignored. `row_length`: each aligned group of 8 block rows holds at least one row with 16 used slots.
All inputs are finite; a program needn't handle non-finite values.
Results may differ from a plain program's by a relative error of at most 0.0075.
Values may be sent and summed in bfloat16 or wider, within the bound.
A program may use at most 64 MiB of HBM per device.

v0:
```python
import jax
import jax.numpy as jnp
from jax import lax
from jax.sharding import PartitionSpec as P

ITERS = 3


def from_behind(block, axis, distance):
    devices = range(lax.axis_size(axis))
    route = [((i - distance) % len(devices), i) for i in devices]
    return lax.ppermute(block, axis, route)


def extended_2(shard, sides, width):
    for axis, dim in sides:
        devices, length = (lax.axis_size(axis), shard.shape[dim])
        up = [(i, (i + 1) % devices) for i in range(devices)]
        down = [(j, i) for i, j in up]
        last = lax.slice_in_dim(shard, length - width, length, axis=dim)
        first = lax.slice_in_dim(shard, 0, width, axis=dim)
        before = lax.ppermute(last, axis, up)
        after = lax.ppermute(first, axis, down)
        shard = jnp.concatenate([before, shard, after], axis=dim)
    return shard


def shards(targets, ridge, blocks, col_index, row_length):
    rows = col_index.shape[0]
    slots = col_index.shape[1]
    width = blocks.shape[3]
    cols = targets.shape[1]
    total = rows * lax.axis_size("asset")
    start = lax.axis_index("asset") * rows
    used = jnp.arange(slots)[None, :] < row_length[:, None]
    masked_shard = blocks * used[:, :, None, None].astype(jnp.bfloat16)
    local_pos = (col_index - start + rows) % total
    onehot = (local_pos[None, :, :] == jnp.arange(3 * rows, dtype=jnp.int32)[:, None, None]).astype(
        jnp.bfloat16
    )
    own_blocks = lax.all_gather(masked_shard, "rhs", axis=2, tiled=True)
    weave = jnp.einsum(
        "cik,ikab->ciab", onehot, own_blocks, preferred_element_type=jnp.float32
    ).astype(jnp.bfloat16)

    def squares(values):
        return lax.psum(jnp.sum(values * values, axis=0), "asset")

    solution = jnp.zeros_like(targets)
    residual = targets
    direction = targets
    norm_now = squares(residual)
    for step in range(ITERS):
        rounded = direction.astype(jnp.bfloat16)
        operate_extended = extended_2(rounded, (("asset", 0),), rows * width)
        operate_extended = operate_extended.reshape(3 * rows, width, cols)
        picked = jnp.take(operate_extended, local_pos, axis=0)
        forward = jnp.einsum(
            "ikab,ikbn->ian", own_blocks, picked, preferred_element_type=jnp.float32
        )
        slab = jnp.einsum(
            "qjpt,jpu->qtu",
            weave,
            operate_extended[rows : 2 * rows],
            preferred_element_type=jnp.float32,
        )
        from_upper = from_behind(slab[:rows].astype(jnp.bfloat16), "asset", -1).astype(jnp.float32)
        from_lower = from_behind(slab[2 * rows :].astype(jnp.bfloat16), "asset", 1).astype(
            jnp.float32
        )
        backward = slab[rows : 2 * rows] + from_upper + from_lower
        image = ridge[:, None] * direction + 0.5 * (forward + backward).reshape(rows * width, cols)
        curve = lax.psum(jnp.sum(direction * image, axis=0), "asset")
        alpha = norm_now / curve
        solution = solution + alpha * direction
        residual = residual - alpha * image
        norm_next = squares(residual)
        direction = residual + norm_next / norm_now * direction
        norm_now = norm_next
    return (solution, residual)


def solution(mesh):
    return jax.shard_map(
        shards,
        mesh=mesh,
        in_specs=(
            P("asset", "rhs"),
            P("asset"),
            P("asset", None, "rhs", None),
            P("asset", None),
            P("asset"),
        ),
        out_specs=(P("asset", "rhs"), P("asset", "rhs")),
        check_vma=False,
    )
```

profile of v0, /device:TPU:6, one launch (start us, length us, event | category | flops | bytes accessed | tf_op | source)
XLA Modules:
  0.0 875.9 jit_solution(18036171837793183966)
XLA Ops:
  11.1 13.9 %collective-permute-start.1 = (bf16[1024,128]{1,0:T(8,128)(2,1)S(1)}, bf16[1024,128]{1,0:T(8,128)(2,1)S(1)}, u32[]{:S(2)}, u32[]{:S(2)}) collective-permute-start(bf16[1024,128]{1,0:T(8,128)(2,1)S(1)} %convert_element_type.49), channel_id=1, source_target_pairs={{8,0},{16,8},{24,16},{32,24},{40,32},{48,40},{56,48},{64,56},{72,6... | collective-permute-start | bytes 786440 | tf_op jit(solution)/shard_map/ppermute | solution.py:23
  27.7 28.4 %all-gather.2.cloned.1.call-done = bf16[8,16,128,128]{3,2,1,0:T(8,128)(2,1)} async-done(((bf16[8,16,16,128]{3,2,1,0:T(8,128)(2,1)}), bf16[8,16,128,128]{3,2,1,0:T(8,128)(2,1)}) %all-gather.2.cloned.1.call-update) | async-done | bytes 4194320 | tf_op jit(solution)/shard_map/all_gather | solution.py:41
  56.1 8.0 convert_bitcast_fusion
  64.1 9.0 %copy.8 = bf16[24,8,128,128]{2,3,1,0:T(8,128)(2,1)} copy(bf16[24,8,128,128]{3,0,2,1:T(8,128)(2,1)} %convert_bitcast_fusion) | data formatting | bytes 12582912 | tf_op jit(solution)/shard_map/convert_element_type | solution.py:44
  73.1 4.6 fusion.53
  78.4 3.6 collective-permute-start.3
  82.0 6.5 collective-permute-start.2
  88.6 3.1 gather_fusion
  94.4 4.9 fusion.33
  99.6 143.9 %all-reduce = (f32[128]{0:T(128)S(1)}, f32[128]{0:T(128)S(1)}) all-reduce(f32[128]{0:T(128)S(1)} %get-tuple-element.4, f32[128]{0:T(128)S(1)} %get-tuple-element.3), channel_id=1, replica_groups=mesh['asset'=64,'rhs'=8] {'asset'}, use_global_device_ids=true, to_apply=%region_1.2 | all-reduce | flops 256 | bytes 2048 | tf_op jit(solution)/shard_map/psum | solution.py:47
  243.7 138.3 %psum.44 = f32[128]{0:T(128)S(1)} all-reduce(f32[128]{0:T(128)S(1)} %multiply_reduce_fusion.3), channel_id=1, replica_groups=mesh['asset'=64,'rhs'=8] {'asset'}, use_global_device_ids=true, to_apply=%region_5.7 | all-reduce | flops 128 | bytes 1024 | tf_op jit(solution)/shard_map/psum | solution.py:47
  382.2 3.7 collective-permute-start.5
  388.1 5.7 fusion.54
  393.9 3.7 collective-permute-start.7
  397.5 5.7 collective-permute-start.6
  407.0 4.9 fusion.30
  412.1 143.8 %psum.45 = f32[128]{0:T(128)S(1)} all-reduce(f32[128]{0:T(128)S(1)} %multiply_reduce_fusion.2), channel_id=1, replica_groups=mesh['asset'=64,'rhs'=8] {'asset'}, use_global_device_ids=true, to_apply=%region_7.9 | all-reduce | flops 128 | bytes 1024 | tf_op jit(solution)/shard_map/psum | solution.py:73
  556.1 138.0 %psum.46 = f32[128]{0:T(128)S(1)} all-reduce(f32[128]{0:T(128)S(1)} %get-tuple-element.7), channel_id=1, replica_groups=mesh['asset'=64,'rhs'=8] {'asset'}, use_global_device_ids=true, to_apply=%region_9.11 | all-reduce | flops 128 | bytes 1024 | tf_op jit(solution)/shard_map/psum | solution.py:47
  694.1 3.9 collective-permute-start.9
  700.0 5.7 fusion.55
  705.8 3.9 collective-permute-start.11
  709.7 5.3 collective-permute-start.10
  718.8 5.0 fusion.27
  724.1 143.9 %psum.47 = f32[128]{0:T(128)S(1)} all-reduce(f32[128]{0:T(128)S(1)} %multiply_reduce_fusion), channel_id=1, replica_groups=mesh['asset'=64,'rhs'=8] {'asset'}, use_global_device_ids=true, to_apply=%region_11.13 | all-reduce | flops 128 | bytes 1024 | tf_op jit(solution)/shard_map/psum | solution.py:73
  (49 shorter events, 24.5 us)
Async XLA Ops:
  7.2 48.9 %all-gather.2.cloned.1.call-start = ((), (), s32[]{:S(2)}) async-start(), calls=%async_computation | async-start | bytes 4718592 | tf_op jit(solution)/shard_map/all_gather | solution.py:41
  11.1 77.4 %collective-permute-start.1 = (bf16[1024,128]{1,0:T(8,128)(2,1)S(1)}, bf16[1024,128]{1,0:T(8,128)(2,1)S(1)}, u32[]{:S(2)}, u32[]{:S(2)}) collective-permute-start(bf16[1024,128]{1,0:T(8,128)(2,1)S(1)} %convert_element_type.49), channel_id=1, source_target_pairs={{8,0},{16,8},{24,16},{32,24},{40,32},{48,40},{56,48},{64,56},{72,6... | collective-permute-start | bytes 786440 | tf_op jit(solution)/shard_map/ppermute | solution.py:23
  24.9 63.5 %collective-permute-start = (bf16[1024,128]{1,0:T(8,128)(2,1)S(1)}, bf16[1024,128]{1,0:T(8,128)(2,1)S(1)}, u32[]{:S(2)}, u32[]{:S(2)}) collective-permute-start(bf16[1024,128]{1,0:T(8,128)(2,1)S(1)} %convert_element_type.49), channel_id=1, source_target_pairs={{0,8},{8,16},{16,24},{24,32},{32,40},{40,48},{48,56},{56,64},{64,7... | collective-permute-start | bytes 786440 | tf_op jit(solution)/shard_map/ppermute | solution.py:22
  78.4 15.2 %collective-permute-start.3 = (bf16[8,128,128]{2,1,0:T(8,128)(2,1)}, bf16[8,128,128]{2,1,0:T(8,128)(2,1)}, u32[]{:S(2)}, u32[]{:S(2)}) collective-permute-start(bf16[8,128,128]{2,1,0:T(8,128)(2,1)} %get-tuple-element.20), channel_id=1, source_target_pairs={{504,0},{0,8},{8,16},{16,24},{24,32},{32,40},{40,48},{48,56},{56,6... | collective-permute-start | bytes 786440 | tf_op jit(solution)/shard_map/ppermute | solution.py:12
  82.0 12.5 %collective-permute-start.2 = (bf16[8,128,128]{2,1,0:T(8,128)(2,1)S(1)}, bf16[8,128,128]{2,1,0:T(8,128)(2,1)}, u32[]{:S(2)}, u32[]{:S(2)}) collective-permute-start(bf16[8,128,128]{2,1,0:T(8,128)(2,1)S(1)} %get-tuple-element.19), channel_id=1, source_target_pairs={{8,0},{16,8},{24,16},{32,24},{40,32},{48,40},{56,48},{64,56},{72,6... | collective-permute-start | bytes 786440 | tf_op jit(solution)/shard_map/ppermute | solution.py:12
  94.4 4.9 copy-start
  94.4 5.0 copy-start.1
  382.2 21.0 %collective-permute-start.5 = (bf16[1024,128]{1,0:T(8,128)(2,1)S(1)}, bf16[1024,128]{1,0:T(8,128)(2,1)S(1)}, u32[]{:S(2)}, u32[]{:S(2)}) collective-permute-start(bf16[1024,128]{1,0:T(8,128)(2,1)S(1)} %get-tuple-element.9), channel_id=1, source_target_pairs={{8,0},{16,8},{24,16},{32,24},{40,32},{48,40},{56,48},{64,56},{72,6... | collective-permute-start | bytes 786440 | tf_op jit(solution)/shard_map/ppermute | solution.py:23
  385.9 17.3 %collective-permute-start.4 = (bf16[1024,128]{1,0:T(8,128)(2,1)S(1)}, bf16[1024,128]{1,0:T(8,128)(2,1)S(1)}, u32[]{:S(2)}, u32[]{:S(2)}) collective-permute-start(bf16[1024,128]{1,0:T(8,128)(2,1)S(1)} %get-tuple-element.9), channel_id=1, source_target_pairs={{0,8},{8,16},{16,24},{24,32},{32,40},{40,48},{48,56},{56,64},{64,7... | collective-permute-start | bytes 786440 | tf_op jit(solution)/shard_map/ppermute | solution.py:22
  393.9 12.6 %collective-permute-start.7 = (bf16[8,128,128]{2,1,0:T(8,128)(2,1)S(1)}, bf16[8,128,128]{2,1,0:T(8,128)(2,1)S(1)}, u32[]{:S(2)}, u32[]{:S(2)}) collective-permute-start(bf16[8,128,128]{2,1,0:T(8,128)(2,1)S(1)} %get-tuple-element.18), channel_id=1, source_target_pairs={{504,0},{0,8},{8,16},{16,24},{24,32},{32,40},{40,48},{48,56},{56,6... | collective-permute-start | bytes 786440 | tf_op jit(solution)/shard_map/ppermute | solution.py:12
  397.5 9.4 %collective-permute-start.6 = (bf16[8,128,128]{2,1,0:T(8,128)(2,1)S(1)}, bf16[8,128,128]{2,1,0:T(8,128)(2,1)S(1)}, u32[]{:S(2)}, u32[]{:S(2)}) collective-permute-start(bf16[8,128,128]{2,1,0:T(8,128)(2,1)S(1)} %get-tuple-element.17), channel_id=1, source_target_pairs={{8,0},{16,8},{24,16},{32,24},{40,32},{48,40},{56,48},{64,56},{72,6... | collective-permute-start | bytes 786440 | tf_op jit(solution)/shard_map/ppermute | solution.py:12
  694.1 20.8 %collective-permute-start.9 = (bf16[1024,128]{1,0:T(8,128)(2,1)S(1)}, bf16[1024,128]{1,0:T(8,128)(2,1)S(1)}, u32[]{:S(2)}, u32[]{:S(2)}) collective-permute-start(bf16[1024,128]{1,0:T(8,128)(2,1)S(1)} %fusion.34), channel_id=1, source_target_pairs={{8,0},{16,8},{24,16},{32,24},{40,32},{48,40},{56,48},{64,56},{72,6... | collective-permute-start | bytes 786440 | tf_op jit(solution)/shard_map/ppermute | solution.py:23
  698.1 16.9 %collective-permute-start.8 = (bf16[1024,128]{1,0:T(8,128)(2,1)S(1)}, bf16[1024,128]{1,0:T(8,128)(2,1)S(1)}, u32[]{:S(2)}, u32[]{:S(2)}) collective-permute-start(bf16[1024,128]{1,0:T(8,128)(2,1)S(1)} %fusion.34), channel_id=1, source_target_pairs={{0,8},{8,16},{16,24},{24,32},{32,40},{40,48},{48,56},{56,64},{64,7... | collective-permute-start | bytes 786440 | tf_op jit(solution)/shard_map/ppermute | solution.py:22
  705.8 12.3 %collective-permute-start.11 = (bf16[8,128,128]{2,1,0:T(8,128)(2,1)S(1)}, bf16[8,128,128]{2,1,0:T(8,128)(2,1)}, u32[]{:S(2)}, u32[]{:S(2)}) collective-permute-start(bf16[8,128,128]{2,1,0:T(8,128)(2,1)S(1)} %get-tuple-element.16), channel_id=1, source_target_pairs={{504,0},{0,8},{8,16},{16,24},{24,32},{32,40},{40,48},{48,56},{56,6... | collective-permute-start | bytes 786440 | tf_op jit(solution)/shard_map/ppermute | solution.py:12
  709.7 9.1 %collective-permute-start.10 = (bf16[8,128,128]{2,1,0:T(8,128)(2,1)S(1)}, bf16[8,128,128]{2,1,0:T(8,128)(2,1)}, u32[]{:S(2)}, u32[]{:S(2)}) collective-permute-start(bf16[8,128,128]{2,1,0:T(8,128)(2,1)S(1)} %get-tuple-element.15), channel_id=1, source_target_pairs={{8,0},{16,8},{24,16},{32,24},{40,32},{48,40},{56,48},{64,56},{72,6... | collective-permute-start | bytes 786440 | tf_op jit(solution)/shard_map/ppermute | solution.py:12
Sparse Core Ops, SparseCore 0:
  10.7 45.3 all-gather.1
where the time goes:
time: 877 us; the launch traced here: 876 us
  blocking collectives  708 us (81%)
  starting transfers between devices  56.1 us (6%)
  matrix products  38.9 us (4%)
  waiting for transfers between devices  32.5 us (4%)
  local copies, waits for them, and re-layouts  19.2 us (2%)
  between operations  14.3 us (2%)
    psum x3, blocking collectives, squares(): return lax.psum(jnp.sum(values * values, axis=0), 'asset')  420 us
    psum x2, blocking collectives, shards(): curve = lax.psum(jnp.sum(direction * image, axis=0), 'asset')  288 us
    ppermute x6, starting transfers between devices, from_behind(): return lax.ppermute(block, axis, route)  28.6 us
    all_gather x1, waiting for transfers between devices, shards(): own_blocks = lax.all_gather(masked_shard, 'rhs', axis=2, tiled=True)  28.4 us
    ppermute x3, starting transfers between devices, extended_2(): after = lax.ppermute(first, axis, down)  21.4 us
  transfers between devices with their start and end apart: 13, of which 5 were waited for; matrix products, arithmetic and copies ran while one was open for 5% of the time, Pallas kernels for 0%

commit v1 on v0

v1 whole, which is shorter than its diff:
```python
import functools

import jax
import jax.numpy as jnp
from jax import lax
from jax.experimental import pallas as pl
from jax.experimental.pallas import tpu as pltpu
from jax.sharding import PartitionSpec as P

ITERS = 3
ROWS = 8
BAND = 2 * ROWS + 1
BS = 128
PAIRS = ROWS // 2
CHUNK = 2 * BAND
SIDE = ROWS + 1
UP_AT = ROWS
DN_AT = CHUNK - SIDE
OWN = PAIRS * CHUNK
PREV_AT = OWN
NEXT_AT = OWN + PAIRS * SIDE
TILES = OWN + 2 * PAIRS * SIDE
PARTS = 8
SUB = BS // PARTS
NX = 4
RING = 8
MESH = pl.DeviceIdType.MESH


def place(row, c):
    low = (c - ROWS + row + CHUNK) % CHUNK
    high = 3 * ROWS + 1 + (ROWS - 1 - row) - c
    pair = jnp.where(row < PAIRS, row, ROWS - 1 - row)
    return pair, jnp.where(row < PAIRS, low, high)


def lanes(tile, count):
    return pl.ds(pl.multiple_of(tile * BS, BS), count * BS)


def kernel(
    pick_ref, mask_ref, targets_ref, ridge_ref, blocks_ref,
    sol_ref, res_ref,
    stored, tiles, band, vec, acc, d, q, w, ridge, red_out, red_in,
    load_sem, send_sem, recv_sem, halo_send, halo_recv, red_send, red_recv,
):
    asset = lax.axis_index("asset")
    part = lax.axis_index("rhs")
    assets = lax.axis_size("asset")
    y, z = asset // RING, asset % RING
    x, core = part // 2, part % 2

    def at_x(step):
        return ((x + step) % NX) * 2 + core

    right, left, far = at_x(1), at_x(NX - 1), at_x(2)
    mate = x * 2 + (1 - core)
    following = (asset + 1) % assets
    preceding = (asset + assets - 1) % assets

    def z_peer(step):
        return y * RING + (z + step) % RING

    def y_peer(step):
        return ((y + step) % RING) * RING + z

    load_blocks = pltpu.make_async_copy(blocks_ref, stored, load_sem.at[0])
    load_targets = pltpu.make_async_copy(targets_ref, res_ref, load_sem.at[1])
    load_blocks.start()
    load_targets.start()

    barrier = pltpu.get_barrier_semaphore()
    greet = [{"rhs": r} for r in (right, left, mate)]
    greet += [{"asset": a} for a in (following, preceding)]
    for step in range(1, RING):
        greet += [{"asset": z_peer(step)}, {"asset": y_peer(step)}]
    for device in greet:
        pl.semaphore_signal(barrier, inc=1, device_id=device, device_id_type=MESH)
    pl.semaphore_wait(barrier, len(greet))

    sent = []

    def copy(index, sems, src, dst, device):
        return pltpu.make_async_remote_copy(
            src_ref=src, dst_ref=dst, send_sem=sems[0].at[index], recv_sem=sems[1].at[index],
            device_id=device, device_id_type=MESH,
        )

    gather = (send_sem, recv_sem)
    KINDS = 23

    def slab(shard, first, count):
        return tiles.at[shard, :, lanes(first, count)]

    def tile_copy(g, kind, shard, first, count, device, to=None):
        to = first if to is None else to
        return copy(g * KINDS + kind, gather, slab(shard, first, count), slab(shard, to, count), device)

    def launch(one):
        one.start()
        sent.append(one)

    def spread(g, source, shard):
        launch(tile_copy(g, 3 + source, shard, g * CHUNK, CHUNK, {"rhs": mate}))
        launch(tile_copy(g, 7 + source, shard, g * CHUNK + UP_AT, SIDE, {"asset": following}, PREV_AT + g * SIDE))
        launch(tile_copy(g, 11 + source, shard, g * CHUNK + DN_AT, SIDE, {"asset": preceding}, NEXT_AT + g * SIDE))

    def land(g, kind, shard, first, count):
        tile_copy(g, kind, shard, first, count, {"rhs": mate}).wait_recv()

    def from_left(g):
        land(g, 0, left, g * CHUNK, CHUNK)
        if g % 2 == 0:
            launch(tile_copy(g, 2, left, g * CHUNK, CHUNK, {"rhs": right}))
        spread(g, 1, left)

    def from_right(g):
        land(g, 1, right, g * CHUNK, CHUNK)
        if g % 2 == 1:
            launch(tile_copy(g, 2, right, g * CHUNK, CHUNK, {"rhs": left}))
        spread(g, 2, right)

    def from_far(g):
        land(g, 2, far, g * CHUNK, CHUNK)
        spread(g, 3, far)

    shards = (part, left, right, far)

    def from_sides(g, source):
        shard = shards[source]
        land(g, 7 + source, shard, PREV_AT + g * SIDE, SIDE)
        launch(tile_copy(g, 15 + source, shard, PREV_AT + g * SIDE, SIDE, {"rhs": mate}))
        land(g, 11 + source, shard, NEXT_AT + g * SIDE, SIDE)
        launch(tile_copy(g, 19 + source, shard, NEXT_AT + g * SIDE, SIDE, {"rhs": mate}))

    def mate_shard(source):
        return ((x + (0, NX - 1, 1, 2)[source]) % NX) * 2 + (1 - core)

    load_blocks.wait()
    for g in range(PAIRS):
        for row in (g, ROWS - 1 - g):

            def densify(c, unused, row=row, g=g):
                pair, at = place(jnp.int32(row), c)
                block = stored[row, pick_ref[row, c]].astype(jnp.float32)
                tiles[part, :, lanes(g * CHUNK + at, 1)] = (block * mask_ref[row, c]).astype(jnp.bfloat16)
                return unused

            lax.fori_loop(0, BAND, densify, 0)
        launch(tile_copy(g, 0, part, g * CHUNK, CHUNK, {"rhs": right}))
        launch(tile_copy(g, 1, part, g * CHUNK, CHUNK, {"rhs": left}))
        spread(g, 0, part)

    def rows(t):
        return pl.ds(pl.multiple_of(t * BS, BS), BS)

    def middle(t):
        return pl.ds(pl.multiple_of((ROWS + t) * BS, BS), BS)

    def halo(step, side):
        length = ROWS * BS
        return copy(
            2 * step + side, (halo_send, halo_recv),
            vec.at[step, pl.ds(length, length), :],
            vec.at[step, pl.ds(2 * length * side, length), :],
            {"asset": (following, preceding)[side]},
        )

    load_targets.wait()

    def round_targets(t, unused):
        vec[0, middle(t), :] = res_ref[rows(t), :].astype(jnp.bfloat16)
        return unused

    lax.fori_loop(0, ROWS, round_targets, 0)
    for side in range(2):
        launch(halo(0, side))

    def spread_ridge(t, unused):
        ridge[rows(t), :] = jnp.broadcast_to(ridge_ref[pl.ds(t, 1), :], (BS, BS)).T
        return unused

    lax.fori_loop(0, ROWS, spread_ridge, 0)

    for g in range(PAIRS):
        from_left(g)
        from_right(g)
        from_sides(g, 0)
        if g >= 1:
            from_far(g - 1)
            from_sides(g - 1, 1)
            from_sides(g - 1, 2)
    from_far(PAIRS - 1)
    from_sides(PAIRS - 1, 1)
    from_sides(PAIRS - 1, 2)
    for g in range(PAIRS):
        from_sides(g, 3)
    for g in range(PAIRS):
        for source in range(4):
            shard = mate_shard(source)
            land(g, 3 + source, shard, g * CHUNK, CHUNK)
            land(g, 15 + source, shard, PREV_AT + g * SIDE, SIDE)
            land(g, 19 + source, shard, NEXT_AT + g * SIDE, SIDE)

    def tile(index):
        return tiles[:, :, lanes(index, 1)].reshape(BS, BS)

    def weave(t, unused):
        def one(c, unused):
            pair, at = place(t, c)
            source = t + c
            row = source % ROWS
            pair_t, at_t = place(row, BAND - 1 - c)
            index = jnp.where(
                source < ROWS,
                PREV_AT + pair_t * SIDE + at_t - UP_AT,
                jnp.where(
                    source < 2 * ROWS,
                    pair_t * CHUNK + at_t,
                    NEXT_AT + pair_t * SIDE + at_t - DN_AT,
                ),
            )
            band[t, :, lanes(t + c, 1)] = tile(pair * CHUNK + at) + tile(index).T
            return unused

        return lax.fori_loop(0, BAND, one, unused)

    lax.fori_loop(0, ROWS, weave, 0)

    def multiply(step, side):
        span = ROWS * BS
        field = vec.at[step, pl.ds(side * span, span), :]
        for t in range(ROWS):
            if side == 0:
                low, high = t, ROWS
            elif side == 1:
                low, high = 0, ROWS
            else:
                low, high = 0, t + 1
            product = jnp.dot(
                band[t, :, side * span + low * BS : side * span + high * BS],
                field[low * BS : high * BS, :],
                preferred_element_type=jnp.float32,
            )
            if side == 1:
                acc[rows(t), :] = product
            else:
                acc[rows(t), :] += product

    def fold(values):
        return jnp.sum(values.reshape(BS // 8, 8, BS), axis=0)

    def total(step, values):
        for phase in range(2):
            red_out[2 * step + phase] = values
            peer = (z_peer, y_peer)[phase]
            base = (2 * step + phase) * (RING - 1)
            copies = [
                copy(base + hop - 1, (red_send, red_recv), red_out.at[2 * step + phase],
                     red_in.at[base + hop - 1], {"asset": peer(hop)})
                for hop in range(1, RING)
            ]
            for one in copies:
                launch(one)
            for one in copies:
                one.wait_recv()
            for hop in range(1, RING):
                values = values + red_in[base + hop - 1]
        return values

    before, curve_before = None, None
    for step in range(ITERS):
        multiply(step, 1)
        for side in range(2):
            halo(step, side).wait_recv()
        multiply(step, 0)
        multiply(step, 2)

        def dots(t, sums, step=step):
            r = res_ref[rows(t), :]
            wt = ridge[rows(t), :] * r + 0.5 * acc[rows(t), :]
            w[rows(t), :] = wt
            out = [sums[0] + fold(r * r), sums[1] + fold(r * wt)]
            if step > 0:
                out.append(sums[2] + fold(r * q[rows(t), :] + d[rows(t), :] * wt))
            return tuple(out)

        count = 2 if step == 0 else 3
        sums = lax.fori_loop(0, ROWS, dots, (jnp.zeros((8, BS), jnp.float32),) * count)
        line = lax.broadcasted_iota(jnp.int32, (8, BS), 0)
        packed = jnp.zeros((8, BS), jnp.float32)
        for i in range(count):
            packed = jnp.where(line == i, jnp.sum(sums[i], axis=0, keepdims=True), packed)
        packed = total(step, packed)
        norm, curve = packed[0:1, :], packed[1:2, :]
        if step > 0:
            beta = norm / before
            curve = curve + beta * (packed[2:3, :] + beta * curve_before)
        alpha = norm / curve
        before, curve_before = norm, curve

        def update(t, unused, step=step):
            r = res_ref[rows(t), :]
            dt, qt = r, w[rows(t), :]
            if step > 0:
                dt = dt + beta * d[rows(t), :]
                qt = qt + beta * q[rows(t), :]
            moved = alpha * dt
            sol_ref[rows(t), :] = moved if step == 0 else sol_ref[rows(t), :] + moved
            r = r - alpha * qt
            res_ref[rows(t), :] = r
            if step < ITERS - 1:
                d[rows(t), :] = dt
                q[rows(t), :] = qt
                vec[step + 1, middle(t), :] = r.astype(jnp.bfloat16)
            return unused

        lax.fori_loop(0, ROWS, update, 0)
        if step < ITERS - 1:
            for side in range(2):
                launch(halo(step + 1, side))

    for one in sent:
        one.wait_send()


def local(targets, ridge, blocks, col_index, row_length):
    slots = col_index.shape[1]
    total = ROWS * lax.axis_size("asset")
    start = lax.axis_index("asset") * ROWS
    here = start + jnp.arange(ROWS, dtype=jnp.int32)[:, None]
    offset = (col_index - here + ROWS + total) % total
    used = jnp.arange(slots, dtype=jnp.int32)[None, :] < row_length[:, None]
    hit = (offset[:, None, :] == jnp.arange(BAND, dtype=jnp.int32)[None, :, None]) & used[:, None, :]
    pick = jnp.sum(jnp.where(hit, jnp.arange(slots, dtype=jnp.int32)[None, None, :], 0), axis=2)
    mask = jnp.sum(hit.astype(jnp.float32), axis=2)

    size = ROWS * BS
    f32 = jnp.float32
    vmem = pl.BlockSpec(memory_space=pltpu.VMEM)
    smem = pl.BlockSpec(memory_space=pltpu.SMEM)
    hbm = pl.BlockSpec(memory_space=pl.ANY)
    kinds = PAIRS * 23
    return pl.pallas_call(
        kernel,
        out_shape=[jax.ShapeDtypeStruct((size, BS), f32)] * 2,
        in_specs=[smem, smem, hbm, vmem, hbm],
        out_specs=[vmem, vmem],
        scratch_shapes=[
            pltpu.VMEM((ROWS, slots, SUB, BS), jnp.bfloat16),
            pltpu.VMEM((PARTS, SUB, TILES * BS), jnp.bfloat16),
            pltpu.VMEM((ROWS, BS, 3 * size), jnp.bfloat16),
            pltpu.VMEM((ITERS, 3 * size, BS), jnp.bfloat16),
            pltpu.VMEM((size, BS), f32),
            pltpu.VMEM((size, BS), f32),
            pltpu.VMEM((size, BS), f32),
            pltpu.VMEM((size, BS), f32),
            pltpu.VMEM((size, BS), f32),
            pltpu.VMEM((2 * ITERS, 8, BS), f32),
            pltpu.VMEM((2 * ITERS * (RING - 1), 8, BS), f32),
            pltpu.SemaphoreType.DMA((2,)),
            pltpu.SemaphoreType.DMA((kinds,)),
            pltpu.SemaphoreType.DMA((kinds,)),
            pltpu.SemaphoreType.DMA((2 * ITERS,)),
            pltpu.SemaphoreType.DMA((2 * ITERS,)),
            pltpu.SemaphoreType.DMA((2 * ITERS * (RING - 1),)),
            pltpu.SemaphoreType.DMA((2 * ITERS * (RING - 1),)),
        ],
        compiler_params=pltpu.CompilerParams(
            collective_id=0, has_side_effects=True, vmem_limit_bytes=60 * 2**20
        ),
    )(pick, mask, targets, ridge.reshape(ROWS, BS), blocks)


def solution(mesh):
    return jax.shard_map(
        local,
        mesh=mesh,
        in_specs=(
            P("asset", "rhs"),
            P("asset"),
            P("asset", None, "rhs", None),
            P("asset", None),
            P("asset"),
        ),
        out_specs=(P("asset", "rhs"), P("asset", "rhs")),
        check_vma=False,
    )
```

time: 877 us -> 109 us (0.12)
  blocking collectives: 708 us -> 0 us
  Pallas kernels: 0 us -> 102 us
  starting transfers between devices: 56.1 us -> 0 us
  matrix products: 38.9 us -> 0 us
  waiting for transfers between devices: 32.5 us -> 0 us
  local copies, waits for them, and re-layouts: 19.2 us -> 3.38 us
  between operations: 14.3 us -> 0.68 us
    psum x5 -> x0, blocking collectives: 708 us -> none  [the longest x3 420 us: squares(): return lax.psum(jnp.sum(values * values, axis=0), 'asset')]
    pallas_call x0 -> x1, Pallas kernels: none -> 102 us  [local(): pl.pallas_call(kernel, out_shape=[jax.ShapeDtypeStruct((size, BS), f32)]...]
    ppermute x12 -> x0, starting transfers between devices: 56 us -> none  [the longest x6 28.6 us: from_behind(): return lax.ppermute(block, axis, route)]
    dot_general x7 -> x0, matrix products: 38.9 us -> none  [the longest x3 16 us: shards(): jnp.einsum('qjpt,jpu->qtu', weave, operate_extended[rows:2 * rows], prefe...]
    all_gather x1 -> x0, waiting for transfers between devices: 28.4 us -> none  [shards(): own_blocks = lax.all_gather(masked_shard, 'rhs', axis=2, tiled=True)]
    gather x3 -> x0, local copies, waits for them, and re-layouts: 9.25 us -> none  [shards(): picked = jnp.take(operate_extended, local_pos, axis=0)]
    convert_element_type x1 -> x0, local copies, waits for them, and re-layouts: 9.03 us -> none  [shards(): weave = jnp.einsum('cik,ikab->ciab', onehot, own_blocks, preferred_elemen...]
  transfers between devices with their start and end apart: 13 -> 0, of which waited for: 5 -> 0; matrix products, arithmetic and copies ran while one was open for 5% -> 0% of each run, Pallas kernels for 0% -> 0%
where the time goes in v1:
time: 109 us; the launch traced here: 108 us
  Pallas kernels  102 us (94%)
  local copies, waits for them, and re-layouts  3.38 us (3%)
  other arithmetic  1.57 us (1%)
    pallas_call x1, Pallas kernels, local(): pl.pallas_call(kernel, out_shape=[jax.ShapeDtypeStruct((size, BS), f32)]...  102 us
    unnamed x8, local copies, waits for them, and re-layouts  3.38 us

profile of v1, /device:TPU:6, one launch (start us, length us, event | category | flops | bytes accessed | tf_op | source)
XLA Modules:
  0.0 107.9 jit_solution(11149595264338539937)
XLA Ops:
  0.6 0.0 copy-start.1
  0.7 0.0 copy-start.2
  0.7 0.6 copy-done.2
  1.3 0.1 iota_compare_fusion.1
  1.4 0.0 copy-done.1
  1.4 0.1 add_select_fusion
  1.5 0.7 convert_reduce_fusion.mask_ref
  2.2 0.7 select_reduce_fusion.pick_ref
  2.9 102.3 %shard_map.68 = (f32[1024,128]{1,0:T(8,128)}, f32[1024,128]{1,0:T(8,128)}) custom-call(s32[8,17]{1,0:T(8,128)} %select_reduce_fusion.pick_ref, f32[8,17]{1,0:T(8,128)} %convert_reduce_fusion.mask_ref, f32[1024,128]{1,0:T(8,128)} %targets_ref.1, f32[8,128]{1,0:T(8,128)} %bitcast.1, bf16[8,16,16,128]{3,2,1,0:T(8,128)(2,1)} %blocks_ref.1), custom_call_target="tpu_custom_call" | custom-call | tf_op jit(solution)/shard_map/pallas_call | solution.py:344
  105.2 0.0 copy-start
  105.2 1.9 %copy.9 = f32[1024,128]{1,0:T(8,128)} copy(f32[1024,128]{1,0:T(8,128)} %get-tuple-element.4) | data formatting | bytes 1048576
  107.1 0.0 copy-done
  107.2 0.8 copy.10
  (1 shorter events, 0.0 us)
Async XLA Ops:
  0.6 0.8 copy-start.1
  0.7 0.7 copy-start.2
  105.2 1.9 %copy-start = (f32[1024,128]{1,0:T(8,128)S(1)}, f32[1024,128]{1,0:T(8,128)}, u32[]{:S(2)}) copy-start(f32[1024,128]{1,0:T(8,128)} %get-tuple-element.5) | copy-start | bytes 1572868

commit v2 on v1

--- a/solution.py
+++ b/solution.py
@@ -28,10 +28,9 @@
 
 
 def place(row, c):
-    low = (c - ROWS + row + CHUNK) % CHUNK
-    high = 3 * ROWS + 1 + (ROWS - 1 - row) - c
-    pair = jnp.where(row < PAIRS, row, ROWS - 1 - row)
-    return pair, jnp.where(row < PAIRS, low, high)
+    if row < PAIRS:
+        return row, (c - ROWS + row + CHUNK) % CHUNK
+    return ROWS - 1 - row, 3 * ROWS + 1 + (ROWS - 1 - row) - c
 
 
 def lanes(tile, count):
@@ -136,20 +135,20 @@
     def mate_shard(source):
         return ((x + (0, NX - 1, 1, 2)[source]) % NX) * 2 + (1 - core)
 
-    load_blocks.wait()
-    for g in range(PAIRS):
+    def densify(g):
         for row in (g, ROWS - 1 - g):
 
-            def densify(c, unused, row=row, g=g):
-                pair, at = place(jnp.int32(row), c)
+            def one(c, unused, row=row):
+                pair, at = place(row, c)
                 block = stored[row, pick_ref[row, c]].astype(jnp.float32)
                 tiles[part, :, lanes(g * CHUNK + at, 1)] = (block * mask_ref[row, c]).astype(jnp.bfloat16)
                 return unused
 
-            lax.fori_loop(0, BAND, densify, 0)
+            lax.fori_loop(0, BAND, one, 0, unroll=True)
+
+    def send_own(g):
         launch(tile_copy(g, 0, part, g * CHUNK, CHUNK, {"rhs": right}))
         launch(tile_copy(g, 1, part, g * CHUNK, CHUNK, {"rhs": left}))
-        spread(g, 0, part)
 
     def rows(t):
         return pl.ds(pl.multiple_of(t * BS, BS), BS)
@@ -166,6 +165,12 @@
             {"asset": (following, preceding)[side]},
         )
 
+    load_blocks.wait()
+    for g in range(2):
+        densify(g)
+        send_own(g)
+        spread(g, 0, part)
+
     load_targets.wait()
 
     def round_targets(t, unused):
@@ -175,6 +180,9 @@
     lax.fori_loop(0, ROWS, round_targets, 0)
     for side in range(2):
         launch(halo(0, side))
+    for g in range(2, PAIRS):
+        densify(g)
+        spread(g, 0, part)
 
     def spread_ridge(t, unused):
         ridge[rows(t), :] = jnp.broadcast_to(ridge_ref[pl.ds(t, 1), :], (BS, BS)).T
@@ -182,50 +190,126 @@
 
     lax.fori_loop(0, ROWS, spread_ridge, 0)
 
-    for g in range(PAIRS):
-        from_left(g)
-        from_right(g)
-        from_sides(g, 0)
-        if g >= 1:
-            from_far(g - 1)
-            from_sides(g - 1, 1)
-            from_sides(g - 1, 2)
-    from_far(PAIRS - 1)
-    from_sides(PAIRS - 1, 1)
-    from_sides(PAIRS - 1, 2)
-    for g in range(PAIRS):
-        from_sides(g, 3)
+    def tile(index):
+        return tiles[:, :, lanes(index, 1)].reshape(BS, BS)
+
+    def lay(g):
+        for source in range(4):
+            land(g, 3 + source, mate_shard(source), g * CHUNK, CHUNK)
+        for row in (g, ROWS - 1 - g):
+
+            def one(c, unused, row=row):
+                pair, at = place(row, c)
+                band[row, :, lanes(row + c, 1)] = tile(g * CHUNK + at)
+                return unused
+
+            lax.fori_loop(0, BAND, one, 0, unroll=True)
+            acc[row * BS : (row + 1) * BS, :] = whole(row)
+
+    def whole(t):
+        return jnp.dot(
+            band[t, :, t * BS : (t + BAND) * BS], vec[0, t * BS : (t + BAND) * BS, :],
+            preferred_element_type=jnp.float32,
+        )
+
+    def fold(values):
+        return jnp.sum(values.reshape(BS // 8, 8, BS), axis=0)
+
+    def stack(sums):
+        line = lax.broadcasted_iota(jnp.int32, (8, BS), 0)
+        packed = jnp.zeros((8, BS), jnp.float32)
+        for i, one in enumerate(sums):
+            packed = jnp.where(line == i, jnp.sum(one, axis=0, keepdims=True), packed)
+        return packed
+
+    def exchange(step, phase):
+        peer = (y_peer, z_peer)[phase]
+        base = (2 * step + phase) * (RING - 1)
+        return [
+            copy(base + hop - 1, (red_send, red_recv), red_out.at[2 * step + phase],
+                 red_in.at[base + hop - 1], {"asset": peer(hop)})
+            for hop in range(1, RING)
+        ]
+
+    def start_sum(step, phase, values):
+        red_out[2 * step + phase] = values
+        for one in exchange(step, phase):
+            launch(one)
+
+    def end_sum(step, phase):
+        for one in exchange(step, phase):
+            one.wait_recv()
+        values = red_out[2 * step + phase]
+        base = (2 * step + phase) * (RING - 1)
+        for hop in range(1, RING):
+            values = values + red_in[base + hop - 1]
+        return values
+
+    from_left(0)
+    send_own(2)
+    from_right(0)
+    from_left(1)
+    send_own(3)
+    from_right(1)
+    from_sides(0, 0)
+    from_sides(1, 0)
+    from_left(2)
+    from_right(2)
+    from_sides(0, 1)
+    from_sides(0, 2)
+    from_far(0)
+    from_left(3)
+    from_right(3)
+    from_far(1)
+    from_sides(2, 0)
+    from_sides(3, 0)
+    from_sides(1, 1)
+    from_sides(1, 2)
+    for side in range(2):
+        halo(0, side).wait_recv()
+    lay(0)
+    lay(1)
+    from_far(2)
+    from_sides(2, 1)
+    from_sides(2, 2)
+    from_sides(0, 3)
+    from_far(3)
+    from_sides(1, 3)
+    from_sides(3, 1)
+    from_sides(3, 2)
+    lay(2)
+    lay(3)
+
+    def first_dots(t, sums):
+        r = res_ref[rows(t), :]
+        return sums[0] + fold(r * r), sums[1] + fold(r * (ridge[rows(t), :] * r + acc[rows(t), :]))
+
+    start_sum(0, 0, stack(lax.fori_loop(0, ROWS, first_dots, (jnp.zeros((8, BS), jnp.float32),) * 2)))
+    from_sides(2, 3)
+    from_sides(3, 3)
+
+    def turn(row, column, index):
+        band[row, :, lanes(column, 1)] += tile(index).T
+
+    def mirror(t, unused):
+        for source in range(ROWS):
+            pair, at = place(source, ROWS + t - source)
+            turn(t, ROWS + source, pair * CHUNK + at)
+        return unused
+
+    lax.fori_loop(0, ROWS, mirror, 0)
+    start_sum(0, 1, end_sum(0, 0))
+
     for g in range(PAIRS):
         for source in range(4):
             shard = mate_shard(source)
-            land(g, 3 + source, shard, g * CHUNK, CHUNK)
             land(g, 15 + source, shard, PREV_AT + g * SIDE, SIDE)
             land(g, 19 + source, shard, NEXT_AT + g * SIDE, SIDE)
-
-    def tile(index):
-        return tiles[:, :, lanes(index, 1)].reshape(BS, BS)
-
-    def weave(t, unused):
-        def one(c, unused):
-            pair, at = place(t, c)
-            source = t + c
-            row = source % ROWS
-            pair_t, at_t = place(row, BAND - 1 - c)
-            index = jnp.where(
-                source < ROWS,
-                PREV_AT + pair_t * SIDE + at_t - UP_AT,
-                jnp.where(
-                    source < 2 * ROWS,
-                    pair_t * CHUNK + at_t,
-                    NEXT_AT + pair_t * SIDE + at_t - DN_AT,
-                ),
-            )
-            band[t, :, lanes(t + c, 1)] = tile(pair * CHUNK + at) + tile(index).T
-            return unused
-
-        return lax.fori_loop(0, BAND, one, unused)
-
-    lax.fori_loop(0, ROWS, weave, 0)
+        for m in range(SIDE):
+            source, t = (g, m) if m <= g else (ROWS - 1 - g, ROWS - m)
+            turn(t, source, PREV_AT + g * SIDE + m)
+            source, t = (ROWS - 1 - g, ROWS - 1 - m) if m <= g else (g, m - 1)
+            turn(t, 2 * ROWS + source, NEXT_AT + g * SIDE + m)
 
     def multiply(step, side):
         span = ROWS * BS
@@ -247,51 +331,32 @@
             else:
                 acc[rows(t), :] += product
 
-    def fold(values):
-        return jnp.sum(values.reshape(BS // 8, 8, BS), axis=0)
-
-    def total(step, values):
-        for phase in range(2):
-            red_out[2 * step + phase] = values
-            peer = (z_peer, y_peer)[phase]
-            base = (2 * step + phase) * (RING - 1)
-            copies = [
-                copy(base + hop - 1, (red_send, red_recv), red_out.at[2 * step + phase],
-                     red_in.at[base + hop - 1], {"asset": peer(hop)})
-                for hop in range(1, RING)
-            ]
-            for one in copies:
-                launch(one)
-            for one in copies:
-                one.wait_recv()
-            for hop in range(1, RING):
-                values = values + red_in[base + hop - 1]
-        return values
-
     before, curve_before = None, None
     for step in range(ITERS):
-        multiply(step, 1)
-        for side in range(2):
-            halo(step, side).wait_recv()
-        multiply(step, 0)
-        multiply(step, 2)
-
-        def dots(t, sums, step=step):
-            r = res_ref[rows(t), :]
-            wt = ridge[rows(t), :] * r + 0.5 * acc[rows(t), :]
-            w[rows(t), :] = wt
-            out = [sums[0] + fold(r * r), sums[1] + fold(r * wt)]
-            if step > 0:
-                out.append(sums[2] + fold(r * q[rows(t), :] + d[rows(t), :] * wt))
-            return tuple(out)
-
-        count = 2 if step == 0 else 3
-        sums = lax.fori_loop(0, ROWS, dots, (jnp.zeros((8, BS), jnp.float32),) * count)
-        line = lax.broadcasted_iota(jnp.int32, (8, BS), 0)
-        packed = jnp.zeros((8, BS), jnp.float32)
-        for i in range(count):
-            packed = jnp.where(line == i, jnp.sum(sums[i], axis=0, keepdims=True), packed)
-        packed = total(step, packed)
+        if step == 0:
+            for t in range(ROWS):
+                w[rows(t), :] = ridge[rows(t), :] * res_ref[rows(t), :] + 0.5 * whole(t)
+            packed = end_sum(0, 1)
+        else:
+            multiply(step, 1)
+            for side in range(2):
+                halo(step, side).wait_recv()
+            multiply(step, 0)
+            multiply(step, 2)
+
+            def dots(t, sums):
+                r = res_ref[rows(t), :]
+                wt = ridge[rows(t), :] * r + 0.5 * acc[rows(t), :]
+                w[rows(t), :] = wt
+                return (
+                    sums[0] + fold(r * r),
+                    sums[1] + fold(r * wt),
+                    sums[2] + fold(r * q[rows(t), :] + d[rows(t), :] * wt),
+                )
+
+            start_sum(step, 0, stack(lax.fori_loop(0, ROWS, dots, (jnp.zeros((8, BS), jnp.float32),) * 3)))
+            start_sum(step, 1, end_sum(step, 0))
+            packed = end_sum(step, 1)
         norm, curve = packed[0:1, :], packed[1:2, :]
         if step > 0:
             beta = norm / before

time: 109 us -> 92.6 us (0.85)
  Pallas kernels: 102 us -> 86.8 us
    pallas_call x1, Pallas kernels: 102 us -> 86.8 us  [local(): pl.pallas_call(kernel, out_shape=[jax.ShapeDtypeStruct((size, BS), f32)]...]
where the time goes in v2:
time: 92.6 us; the launch traced here: 92.4 us
  Pallas kernels  86.8 us (94%)
  local copies, waits for them, and re-layouts  3.38 us (4%)
  other arithmetic  1.57 us (2%)
    pallas_call x1, Pallas kernels, local(): pl.pallas_call(kernel, out_shape=[jax.ShapeDtypeStruct((size, BS), f32)]...  86.8 us
    unnamed x8, local copies, waits for them, and re-layouts  3.38 us

profile of v2, /device:TPU:6, one launch (start us, length us, event | category | flops | bytes accessed | tf_op | source)
XLA Modules:
  0.0 92.4 jit_solution(16156851432692188386)
XLA Ops:
  0.6 0.0 copy-start.1
  0.7 0.0 copy-start.2
  0.7 0.6 copy-done.2
  1.3 0.1 iota_compare_fusion.1
  1.4 0.0 copy-done.1
  1.4 0.1 add_select_fusion
  1.5 0.7 convert_reduce_fusion.mask_ref
  2.2 0.7 select_reduce_fusion.pick_ref
  2.9 86.8 %shard_map.68 = (f32[1024,128]{1,0:T(8,128)}, f32[1024,128]{1,0:T(8,128)}) custom-call(s32[8,17]{1,0:T(8,128)} %select_reduce_fusion.pick_ref, f32[8,17]{1,0:T(8,128)} %convert_reduce_fusion.mask_ref, f32[1024,128]{1,0:T(8,128)} %targets_ref.1, f32[8,128]{1,0:T(8,128)} %bitcast.1, bf16[8,16,16,128]{3,2,1,0:T(8,128)(2,1)} %blocks_ref.1), custom_call_target="tpu_custom_call" | custom-call | tf_op jit(solution)/shard_map/pallas_call | solution.py:409
  89.7 0.0 copy-start
  89.7 1.9 %copy.9 = f32[1024,128]{1,0:T(8,128)} copy(f32[1024,128]{1,0:T(8,128)} %get-tuple-element.4) | data formatting | bytes 1048576
  91.6 0.0 copy-done
  91.6 0.8 copy.10
  (1 shorter events, 0.0 us)
Async XLA Ops:
  0.6 0.8 copy-start.1
  0.7 0.7 copy-start.2
  89.7 1.9 %copy-start = (f32[1024,128]{1,0:T(8,128)S(1)}, f32[1024,128]{1,0:T(8,128)}, u32[]{:S(2)}) copy-start(f32[1024,128]{1,0:T(8,128)} %get-tuple-element.5) | copy-start | bytes 1572868

commit v3 on v2

--- a/solution.py
+++ b/solution.py
@@ -20,6 +20,8 @@
 PREV_AT = OWN
 NEXT_AT = OWN + PAIRS * SIDE
 TILES = OWN + 2 * PAIRS * SIDE
+PIECE = 2
+PIECES = ROWS // PIECE
 PARTS = 8
 SUB = BS // PARTS
 NX = 4
@@ -38,9 +40,9 @@
 
 
 def kernel(
-    pick_ref, mask_ref, targets_ref, ridge_ref, blocks_ref,
-    sol_ref, res_ref,
-    stored, tiles, band, vec, acc, d, q, w, ridge, red_out, red_in,
+    col_ref, length_ref, targets_ref, ridge_ref, blocks_ref,
+    sol_ref, res_ref, d, q, w, coef_ref,
+    col, length, slot, stored, tiles, band, vec, acc, ridge_rows, ridge, red_out, red_in,
     load_sem, send_sem, recv_sem, halo_send, halo_recv, red_send, red_recv,
 ):
     asset = lax.axis_index("asset")
@@ -65,8 +67,14 @@
 
     load_blocks = pltpu.make_async_copy(blocks_ref, stored, load_sem.at[0])
     load_targets = pltpu.make_async_copy(targets_ref, res_ref, load_sem.at[1])
+    load_col = pltpu.make_async_copy(col_ref, col, load_sem.at[2])
+    load_length = pltpu.make_async_copy(length_ref, length, load_sem.at[3])
+    load_ridge = pltpu.make_async_copy(ridge_ref, ridge_rows, load_sem.at[4])
+    load_col.start()
+    load_length.start()
     load_blocks.start()
     load_targets.start()
+    load_ridge.start()
 
     barrier = pltpu.get_barrier_semaphore()
     greet = [{"rhs": r} for r in (right, left, mate)]
@@ -75,6 +83,28 @@
         greet += [{"asset": z_peer(step)}, {"asset": y_peer(step)}]
     for device in greet:
         pl.semaphore_signal(barrier, inc=1, device_id=device, device_id_type=MESH)
+
+    load_col.wait()
+    load_length.wait()
+    slots = col.shape[1]
+    blocks_in_all = assets * ROWS
+
+    def find(row, unused):
+        here = asset * ROWS + row - ROWS
+        offsets = []
+        for k in range(slots):
+            offset = col[row, k] - here
+            offset = jnp.where(offset < 0, offset + blocks_in_all, offset)
+            offset = jnp.where(offset >= blocks_in_all, offset - blocks_in_all, offset)
+            offsets.append(jnp.where(k < length[row], offset, -1))
+        for c in range(BAND):
+            found = jnp.int32(0)
+            for k in range(slots):
+                found = jnp.where(offsets[k] == c, k + 1, found)
+            slot[row, c] = found
+        return unused
+
+    lax.fori_loop(0, ROWS, find, 0)
     pl.semaphore_wait(barrier, len(greet))
 
     sent = []
@@ -140,8 +170,10 @@
 
             def one(c, unused, row=row):
                 pair, at = place(row, c)
-                block = stored[row, pick_ref[row, c]].astype(jnp.float32)
-                tiles[part, :, lanes(g * CHUNK + at, 1)] = (block * mask_ref[row, c]).astype(jnp.bfloat16)
+                found = slot[row, c]
+                block = stored[row, jnp.maximum(found - 1, 0)].astype(jnp.float32)
+                keep = jnp.minimum(found, 1).astype(jnp.float32)
+                tiles[part, :, lanes(g * CHUNK + at, 1)] = (block * keep).astype(jnp.bfloat16)
                 return unused
 
             lax.fori_loop(0, BAND, one, 0, unroll=True)
@@ -156,12 +188,12 @@
     def middle(t):
         return pl.ds(pl.multiple_of((ROWS + t) * BS, BS), BS)
 
-    def halo(step, side):
-        length = ROWS * BS
+    def halo(step, side, piece):
+        span, at = ROWS * BS, piece * PIECE * BS
         return copy(
-            2 * step + side, (halo_send, halo_recv),
-            vec.at[step, pl.ds(length, length), :],
-            vec.at[step, pl.ds(2 * length * side, length), :],
+            (2 * step + side) * PIECES + piece, (halo_send, halo_recv),
+            vec.at[step, pl.ds(span + at, PIECE * BS), :],
+            vec.at[step, pl.ds(2 * span * side + at, PIECE * BS), :],
             {"asset": (following, preceding)[side]},
         )
 
@@ -178,17 +210,24 @@
         return unused
 
     lax.fori_loop(0, ROWS, round_targets, 0)
-    for side in range(2):
-        launch(halo(0, side))
+    for piece in range(PIECES):
+        for side in range(2):
+            launch(halo(0, side, piece))
     for g in range(2, PAIRS):
         densify(g)
         spread(g, 0, part)
 
     def spread_ridge(t, unused):
-        ridge[rows(t), :] = jnp.broadcast_to(ridge_ref[pl.ds(t, 1), :], (BS, BS)).T
+        ridge[rows(t), :] = jnp.broadcast_to(ridge_rows[pl.ds(t, 1), :], (BS, BS)).T
         return unused
 
+    load_ridge.wait()
     lax.fori_loop(0, ROWS, spread_ridge, 0)
+    for t in range(0, ROWS, PIECE):
+        for low in range(PIECE):
+            for high in range(low + 1, PIECE):
+                band[t + high, :, lanes(t + low, 1)] = jnp.zeros((BS, BS), jnp.bfloat16)
+                band[t + low, :, lanes(2 * ROWS + t + high, 1)] = jnp.zeros((BS, BS), jnp.bfloat16)
 
     def tile(index):
         return tiles[:, :, lanes(index, 1)].reshape(BS, BS)
@@ -255,28 +294,21 @@
     from_sides(1, 0)
     from_left(2)
     from_right(2)
-    from_sides(0, 1)
-    from_sides(0, 2)
     from_far(0)
     from_left(3)
     from_right(3)
     from_far(1)
     from_sides(2, 0)
     from_sides(3, 0)
-    from_sides(1, 1)
-    from_sides(1, 2)
-    for side in range(2):
-        halo(0, side).wait_recv()
+    from_sides(0, 1)
+    from_sides(0, 2)
+    for piece in range(PIECES):
+        for side in range(2):
+            halo(0, side, piece).wait_recv()
     lay(0)
     lay(1)
     from_far(2)
-    from_sides(2, 1)
-    from_sides(2, 2)
-    from_sides(0, 3)
     from_far(3)
-    from_sides(1, 3)
-    from_sides(3, 1)
-    from_sides(3, 2)
     lay(2)
     lay(3)
 
@@ -285,8 +317,8 @@
         return sums[0] + fold(r * r), sums[1] + fold(r * (ridge[rows(t), :] * r + acc[rows(t), :]))
 
     start_sum(0, 0, stack(lax.fori_loop(0, ROWS, first_dots, (jnp.zeros((8, BS), jnp.float32),) * 2)))
-    from_sides(2, 3)
-    from_sides(3, 3)
+    for g, source in ((1, 1), (1, 2), (2, 1), (2, 2), (0, 3)):
+        from_sides(g, source)
 
     def turn(row, column, index):
         band[row, :, lanes(column, 1)] += tile(index).T
@@ -297,8 +329,13 @@
             turn(t, ROWS + source, pair * CHUNK + at)
         return unused
 
-    lax.fori_loop(0, ROWS, mirror, 0)
+    lax.fori_loop(0, PAIRS, mirror, 0)
+    for g, source in ((3, 1), (3, 2), (1, 3)):
+        from_sides(g, source)
     start_sum(0, 1, end_sum(0, 0))
+    for g, source in ((2, 3), (3, 3)):
+        from_sides(g, source)
+    lax.fori_loop(PAIRS, ROWS, mirror, 0)
 
     for g in range(PAIRS):
         for source in range(4):
@@ -311,25 +348,14 @@
             source, t = (ROWS - 1 - g, ROWS - 1 - m) if m <= g else (g, m - 1)
             turn(t, 2 * ROWS + source, NEXT_AT + g * SIDE + m)
 
-    def multiply(step, side):
-        span = ROWS * BS
-        field = vec.at[step, pl.ds(side * span, span), :]
-        for t in range(ROWS):
-            if side == 0:
-                low, high = t, ROWS
-            elif side == 1:
-                low, high = 0, ROWS
-            else:
-                low, high = 0, t + 1
-            product = jnp.dot(
-                band[t, :, side * span + low * BS : side * span + high * BS],
-                field[low * BS : high * BS, :],
-                preferred_element_type=jnp.float32,
-            )
-            if side == 1:
-                acc[rows(t), :] = product
-            else:
-                acc[rows(t), :] += product
+    span = ROWS * BS
+
+    def product(step, first, last, column, count):
+        left = band[first:last, :, column * BS : (column + count) * BS]
+        return jnp.dot(
+            left.reshape((last - first) * BS, count * BS), vec[step, column * BS : (column + count) * BS, :],
+            preferred_element_type=jnp.float32,
+        )
 
     before, curve_before = None, None
     for step in range(ITERS):
@@ -338,11 +364,14 @@
                 w[rows(t), :] = ridge[rows(t), :] * res_ref[rows(t), :] + 0.5 * whole(t)
             packed = end_sum(0, 1)
         else:
-            multiply(step, 1)
-            for side in range(2):
-                halo(step, side).wait_recv()
-            multiply(step, 0)
-            multiply(step, 2)
+            for t in range(ROWS):
+                acc[rows(t), :] = product(step, t, t + 1, ROWS, ROWS)
+            for piece in range(PIECES):
+                at = piece * PIECE
+                halo(step, 0, piece).wait_recv()
+                acc[0 : (at + PIECE) * BS, :] += product(step, 0, at + PIECE, at, PIECE)
+                halo(step, 1, piece).wait_recv()
+                acc[at * BS :, :] += product(step, at, ROWS, 2 * ROWS + at, PIECE)
 
             def dots(t, sums):
                 r = res_ref[rows(t), :]
@@ -363,6 +392,10 @@
             curve = curve + beta * (packed[2:3, :] + beta * curve_before)
         alpha = norm / curve
         before, curve_before = norm, curve
+
+        if step == ITERS - 1:
+            coef_ref[...] = jnp.concatenate([alpha, beta, jnp.zeros((6, BS), jnp.float32)], axis=0)
+            break
 
         def update(t, unused, step=step):
             r = res_ref[rows(t), :]
@@ -374,16 +407,15 @@
             sol_ref[rows(t), :] = moved if step == 0 else sol_ref[rows(t), :] + moved
             r = r - alpha * qt
             res_ref[rows(t), :] = r
-            if step < ITERS - 1:
-                d[rows(t), :] = dt
-                q[rows(t), :] = qt
-                vec[step + 1, middle(t), :] = r.astype(jnp.bfloat16)
+            d[rows(t), :] = dt
+            q[rows(t), :] = qt
+            vec[step + 1, middle(t), :] = r.astype(jnp.bfloat16)
             return unused
 
-        lax.fori_loop(0, ROWS, update, 0)
-        if step < ITERS - 1:
+        for piece in range(PIECES):
+            lax.fori_loop(piece * PIECE, (piece + 1) * PIECE, update, 0)
             for side in range(2):
-                launch(halo(step + 1, side))
+                launch(halo(step + 1, side, piece))
 
     for one in sent:
         one.wait_send()
@@ -391,50 +423,45 @@
 
 def local(targets, ridge, blocks, col_index, row_length):
     slots = col_index.shape[1]
-    total = ROWS * lax.axis_size("asset")
-    start = lax.axis_index("asset") * ROWS
-    here = start + jnp.arange(ROWS, dtype=jnp.int32)[:, None]
-    offset = (col_index - here + ROWS + total) % total
-    used = jnp.arange(slots, dtype=jnp.int32)[None, :] < row_length[:, None]
-    hit = (offset[:, None, :] == jnp.arange(BAND, dtype=jnp.int32)[None, :, None]) & used[:, None, :]
-    pick = jnp.sum(jnp.where(hit, jnp.arange(slots, dtype=jnp.int32)[None, None, :], 0), axis=2)
-    mask = jnp.sum(hit.astype(jnp.float32), axis=2)
-
     size = ROWS * BS
     f32 = jnp.float32
     vmem = pl.BlockSpec(memory_space=pltpu.VMEM)
-    smem = pl.BlockSpec(memory_space=pltpu.SMEM)
-    hbm = pl.BlockSpec(memory_space=pl.ANY)
+    hbm = pl.BlockSpec(memory_space=pltpu.HBM)
     kinds = PAIRS * 23
-    return pl.pallas_call(
+    field = jax.ShapeDtypeStruct((size, BS), f32)
+    operands = (col_index, row_length, targets, ridge.reshape(ROWS, BS), blocks)
+    solution, residual, d, q, w, coef = pl.pallas_call(
         kernel,
-        out_shape=[jax.ShapeDtypeStruct((size, BS), f32)] * 2,
-        in_specs=[smem, smem, hbm, vmem, hbm],
-        out_specs=[vmem, vmem],
+        out_shape=[field] * 5 + [jax.ShapeDtypeStruct((8, BS), f32)],
+        in_specs=[hbm] * 5,
+        out_specs=[vmem] * 6,
         scratch_shapes=[
+            pltpu.SMEM((ROWS, slots), jnp.int32),
+            pltpu.SMEM((ROWS,), jnp.int32),
+            pltpu.SMEM((ROWS, BAND), jnp.int32),
             pltpu.VMEM((ROWS, slots, SUB, BS), jnp.bfloat16),
             pltpu.VMEM((PARTS, SUB, TILES * BS), jnp.bfloat16),
             pltpu.VMEM((ROWS, BS, 3 * size), jnp.bfloat16),
             pltpu.VMEM((ITERS, 3 * size, BS), jnp.bfloat16),
             pltpu.VMEM((size, BS), f32),
-            pltpu.VMEM((size, BS), f32),
-            pltpu.VMEM((size, BS), f32),
-            pltpu.VMEM((size, BS), f32),
+            pltpu.VMEM((ROWS, BS), f32),
             pltpu.VMEM((size, BS), f32),
             pltpu.VMEM((2 * ITERS, 8, BS), f32),
             pltpu.VMEM((2 * ITERS * (RING - 1), 8, BS), f32),
-            pltpu.SemaphoreType.DMA((2,)),
+            pltpu.SemaphoreType.DMA((5,)),
             pltpu.SemaphoreType.DMA((kinds,)),
             pltpu.SemaphoreType.DMA((kinds,)),
-            pltpu.SemaphoreType.DMA((2 * ITERS,)),
-            pltpu.SemaphoreType.DMA((2 * ITERS,)),
+            pltpu.SemaphoreType.DMA((2 * ITERS * PIECES,)),
+            pltpu.SemaphoreType.DMA((2 * ITERS * PIECES,)),
             pltpu.SemaphoreType.DMA((2 * ITERS * (RING - 1),)),
             pltpu.SemaphoreType.DMA((2 * ITERS * (RING - 1),)),
         ],
         compiler_params=pltpu.CompilerParams(
-            collective_id=0, has_side_effects=True, vmem_limit_bytes=60 * 2**20
+            collective_id=0, has_side_effects=True, vmem_limit_bytes=36 * 2**20
         ),
-    )(pick, mask, targets, ridge.reshape(ROWS, BS), blocks)
+    )(*(pltpu.with_memory_space_constraint(one, pltpu.HBM) for one in operands))
+    alpha, beta = coef[0:1], coef[1:2]
+    return solution + alpha * (residual + beta * d), residual - alpha * (w + beta * q)
 
 
 def solution(mesh):

time: 92.6 us -> 86 us (0.929)
  local copies, waits for them, and re-layouts: 3.38 us -> 0.01 us
  Pallas kernels: 86.8 us -> 84.1 us
    unnamed x8 -> x0, local copies, waits for them, and re-layouts: 3.38 us -> none
    pallas_call x1, Pallas kernels: 86.8 us -> 84.1 us  [local(): pl.pallas_call(kernel, out_shape=[field] * 5 + [jax.ShapeDtypeStruct((8,...]
    reduce_sum x2 -> x0, other arithmetic: 1.41 us -> none  [the longest x1 0.71 us: local(): mask = jnp.sum(hit.astype(jnp.float32), axis=2)]
    sub x0 -> x1, other arithmetic: none -> 1.11 us  [local(): residual - alpha * (w + beta * q)]
where the time goes in v3:
time: 86 us; the launch traced here: 85.8 us
  Pallas kernels  84.1 us (98%)
  other arithmetic  1.11 us (1%)
    pallas_call x1, Pallas kernels, local(): pl.pallas_call(kernel, out_shape=[field] * 5 + [jax.ShapeDtypeStruct((8,...  84.1 us

profile of v3, /device:TPU:6, one launch (start us, length us, event | category | flops | bytes accessed | tf_op | source)
XLA Modules:
  0.0 85.8 jit_solution(3911017447241672589)
XLA Ops:
  0.6 84.1 %shard_map.68 = (f32[1024,128]{1,0:T(8,128)S(1)}, f32[1024,128]{1,0:T(8,128)S(1)}, f32[1024,128]{1,0:T(8,128)S(1)}, f32[1024,128]{1,0:T(8,128)S(1)}, f32[1024,128]{1,0:T(8,128)S(1)}, /*index=5*/f32[8,128]{1,0:T(8,128)S(1)}) custom-call(s32[8,16]{1,0:T(8,128)} %col_ref.1, s32[8]{0:T(128)} %length_ref.1, f32[1024,128]{1,0:T(8,128)} %targets_ref.1, ...), custom_call_target="tpu_custom_call" | custom-call | tf_op jit(solution)/shard_map/pallas_call | solution.py:433
  84.7 1.1 %multiply_subtract_fusion = (f32[1024,128]{1,0:T(8,128)}, f32[1024,128]{1,0:T(8,128)}) fusion(f32[1024,128]{1,0:T(8,128)S(1)} %get-tuple-element.10, f32[1024,128]{1,0:T(8,128)S(1)} %get-tuple-element.12, f32[1024,128]{1,0:T(8,128)S(1)} %get-tuple-element.13, f32[128]{0:T(128)S(1)} %get-tuple-element.17, f32[128]{0:T(128)S(1)} %get-tuple-element.16, ...), kind=kLoop, calls=%fused_computation | loop fusion | flops 1048576 | bytes 3671040 | tf_op jit(solution)/shard_map/sub | solution.py:464
  (1 shorter events, 0.0 us)

commit v4 on v3

--- a/solution.py
+++ b/solution.py
@@ -42,7 +42,7 @@
 def kernel(
     col_ref, length_ref, targets_ref, ridge_ref, blocks_ref,
     sol_ref, res_ref, d, q, w, coef_ref,
-    col, length, slot, stored, tiles, band, vec, acc, ridge_rows, ridge, red_out, red_in,
+    col, length, slot, stored, tiles, band, vec, pull, acc, ridge_rows, ridge, red_out, red_in,
     load_sem, send_sem, recv_sem, halo_send, halo_recv, red_send, red_recv,
 ):
     asset = lax.axis_index("asset")
@@ -69,7 +69,7 @@
     load_targets = pltpu.make_async_copy(targets_ref, res_ref, load_sem.at[1])
     load_col = pltpu.make_async_copy(col_ref, col, load_sem.at[2])
     load_length = pltpu.make_async_copy(length_ref, length, load_sem.at[3])
-    load_ridge = pltpu.make_async_copy(ridge_ref, ridge_rows, load_sem.at[4])
+    load_ridge = pltpu.make_async_copy(ridge_ref, ridge_rows.at[1], load_sem.at[4])
     load_col.start()
     load_length.start()
     load_blocks.start()
@@ -190,13 +190,23 @@
 
     def halo(step, side, piece):
         span, at = ROWS * BS, piece * PIECE * BS
+        field = vec.at[0] if step == 0 else pull.at[step - 1]
         return copy(
             (2 * step + side) * PIECES + piece, (halo_send, halo_recv),
-            vec.at[step, pl.ds(span + at, PIECE * BS), :],
-            vec.at[step, pl.ds(2 * span * side + at, PIECE * BS), :],
+            field.at[pl.ds(span + at, PIECE * BS), :],
+            field.at[pl.ds(2 * span * side + at, PIECE * BS), :],
             {"asset": (following, preceding)[side]},
         )
 
+    def ridge_halo(side):
+        return copy(
+            2 * ITERS * PIECES + side, (halo_send, halo_recv), ridge_rows.at[1], ridge_rows.at[2 * side],
+            {"asset": (following, preceding)[side]},
+        )
+
+    load_ridge.wait()
+    for side in range(2):
+        launch(ridge_halo(side))
     load_blocks.wait()
     for g in range(2):
         densify(g)
@@ -218,16 +228,11 @@
         spread(g, 0, part)
 
     def spread_ridge(t, unused):
-        ridge[rows(t), :] = jnp.broadcast_to(ridge_rows[pl.ds(t, 1), :], (BS, BS)).T
+        line = ridge_rows[t // ROWS, pl.ds(t % ROWS, 1), :]
+        ridge[rows(t), :] = jnp.broadcast_to(line, (BS, BS)).T
         return unused
 
-    load_ridge.wait()
-    lax.fori_loop(0, ROWS, spread_ridge, 0)
-    for t in range(0, ROWS, PIECE):
-        for low in range(PIECE):
-            for high in range(low + 1, PIECE):
-                band[t + high, :, lanes(t + low, 1)] = jnp.zeros((BS, BS), jnp.bfloat16)
-                band[t + low, :, lanes(2 * ROWS + t + high, 1)] = jnp.zeros((BS, BS), jnp.bfloat16)
+    lax.fori_loop(ROWS, 2 * ROWS, spread_ridge, 0)
 
     def tile(index):
         return tiles[:, :, lanes(index, 1)].reshape(BS, BS)
@@ -243,11 +248,11 @@
                 return unused
 
             lax.fori_loop(0, BAND, one, 0, unroll=True)
-            acc[row * BS : (row + 1) * BS, :] = whole(row)
-
-    def whole(t):
+            acc[row * BS : (row + 1) * BS, :] = whole(0, row)
+
+    def whole(step, t):
         return jnp.dot(
-            band[t, :, t * BS : (t + BAND) * BS], vec[0, t * BS : (t + BAND) * BS, :],
+            band[t, :, t * BS : (t + BAND) * BS], vec[step, t * BS : (t + BAND) * BS, :],
             preferred_element_type=jnp.float32,
         )
 
@@ -262,7 +267,7 @@
         return packed
 
     def exchange(step, phase):
-        peer = (y_peer, z_peer)[phase]
+        peer = ((y_peer, z_peer) if step == 0 else (z_peer, y_peer))[phase]
         base = (2 * step + phase) * (RING - 1)
         return [
             copy(base + hop - 1, (red_send, red_recv), red_out.at[2 * step + phase],
@@ -292,6 +297,10 @@
     from_right(1)
     from_sides(0, 0)
     from_sides(1, 0)
+    for side in range(2):
+        ridge_halo(side).wait_recv()
+    lax.fori_loop(0, ROWS, spread_ridge, 0)
+    lax.fori_loop(2 * ROWS, 3 * ROWS, spread_ridge, 0)
     from_left(2)
     from_right(2)
     from_far(0)
@@ -314,7 +323,7 @@
 
     def first_dots(t, sums):
         r = res_ref[rows(t), :]
-        return sums[0] + fold(r * r), sums[1] + fold(r * (ridge[rows(t), :] * r + acc[rows(t), :]))
+        return sums[0] + fold(r * r), sums[1] + fold(r * (ridge[middle(t), :] * r + acc[rows(t), :]))
 
     start_sum(0, 0, stack(lax.fori_loop(0, ROWS, first_dots, (jnp.zeros((8, BS), jnp.float32),) * 2)))
     for g, source in ((1, 1), (1, 2), (2, 1), (2, 2), (0, 3)):
@@ -348,56 +357,60 @@
             source, t = (ROWS - 1 - g, ROWS - 1 - m) if m <= g else (g, m - 1)
             turn(t, 2 * ROWS + source, NEXT_AT + g * SIDE + m)
 
-    span = ROWS * BS
-
-    def product(step, first, last, column, count):
-        left = band[first:last, :, column * BS : (column + count) * BS]
-        return jnp.dot(
-            left.reshape((last - first) * BS, count * BS), vec[step, column * BS : (column + count) * BS, :],
-            preferred_element_type=jnp.float32,
-        )
-
-    before, curve_before = None, None
+    def start_halo(step, piece):
+        for side in range(2):
+            launch(halo(step, side, piece))
+
+    def end_halo(step):
+        for piece in range(PIECES):
+            for side in range(2):
+                halo(step, side, piece).wait_recv()
+
+    def image(step, t):
+        r = res_ref[rows(t), :]
+        part_b = 0.5 * whole(step, t)
+        wt = ridge[middle(t), :] * r + part_b
+        w[rows(t), :] = wt
+        if step < ITERS - 1:
+            pull[step, middle(t), :] = part_b.astype(jnp.bfloat16)
+            if step == 0 and t % PIECE == PIECE - 1:
+                start_halo(1, t // PIECE)
+        return r, wt
+
+    norms, curves, alphas, betas = [], [], [], [None]
     for step in range(ITERS):
         if step == 0:
             for t in range(ROWS):
-                w[rows(t), :] = ridge[rows(t), :] * res_ref[rows(t), :] + 0.5 * whole(t)
+                image(0, t)
             packed = end_sum(0, 1)
         else:
+            sums = [jnp.zeros((8, BS), jnp.float32)] * 3
             for t in range(ROWS):
-                acc[rows(t), :] = product(step, t, t + 1, ROWS, ROWS)
-            for piece in range(PIECES):
-                at = piece * PIECE
-                halo(step, 0, piece).wait_recv()
-                acc[0 : (at + PIECE) * BS, :] += product(step, 0, at + PIECE, at, PIECE)
-                halo(step, 1, piece).wait_recv()
-                acc[at * BS :, :] += product(step, at, ROWS, 2 * ROWS + at, PIECE)
-
-            def dots(t, sums):
-                r = res_ref[rows(t), :]
-                wt = ridge[rows(t), :] * r + 0.5 * acc[rows(t), :]
-                w[rows(t), :] = wt
-                return (
-                    sums[0] + fold(r * r),
-                    sums[1] + fold(r * wt),
-                    sums[2] + fold(r * q[rows(t), :] + d[rows(t), :] * wt),
-                )
-
-            start_sum(step, 0, stack(lax.fori_loop(0, ROWS, dots, (jnp.zeros((8, BS), jnp.float32),) * 3)))
+                r, wt = image(step, t)
+                sums[0] = sums[0] + fold(r * r)
+                sums[1] = sums[1] + fold(r * wt)
+                sums[2] = sums[2] + fold(r * q[rows(t), :] + d[rows(t), :] * wt)
+            start_sum(step, 0, stack(sums))
+            early = 2 if step < ITERS - 1 else 0
+            for piece in range(early):
+                start_halo(step + 1, piece)
             start_sum(step, 1, end_sum(step, 0))
+            for piece in range(early, PIECES if step < ITERS - 1 else 0):
+                start_halo(step + 1, piece)
             packed = end_sum(step, 1)
         norm, curve = packed[0:1, :], packed[1:2, :]
         if step > 0:
-            beta = norm / before
-            curve = curve + beta * (packed[2:3, :] + beta * curve_before)
-        alpha = norm / curve
-        before, curve_before = norm, curve
-
+            betas.append(norm / norms[-1])
+            curve = curve + betas[-1] * (packed[2:3, :] + betas[-1] * curves[-1])
+        norms.append(norm)
+        curves.append(curve)
+        alphas.append(norm / curve)
+        alpha, beta = alphas[-1], betas[-1]
         if step == ITERS - 1:
             coef_ref[...] = jnp.concatenate([alpha, beta, jnp.zeros((6, BS), jnp.float32)], axis=0)
             break
 
-        def update(t, unused, step=step):
+        def update(t, unused, step=step, alpha=alpha, beta=beta):
             r = res_ref[rows(t), :]
             dt, qt = r, w[rows(t), :]
             if step > 0:
@@ -412,10 +425,23 @@
             vec[step + 1, middle(t), :] = r.astype(jnp.bfloat16)
             return unused
 
-        for piece in range(PIECES):
-            lax.fori_loop(piece * PIECE, (piece + 1) * PIECE, update, 0)
-            for side in range(2):
-                launch(halo(step + 1, side, piece))
+        def update_halo(t, unused, step=step):
+            for block in (t, 2 * ROWS + t):
+                at = rows(block)
+                shift = ridge[at, :]
+                r = vec[0, at, :].astype(jnp.float32)
+                move, push = r, pull[0, at, :].astype(jnp.float32)
+                r = r - alphas[0] * (shift * move + push)
+                if step > 0:
+                    move = r + betas[1] * move
+                    push = pull[1, at, :].astype(jnp.float32) + betas[1] * push
+                    r = r - alphas[1] * (shift * move + push)
+                vec[step + 1, at, :] = r.astype(jnp.bfloat16)
+            return unused
+
+        lax.fori_loop(0, ROWS, update, 0)
+        end_halo(step + 1)
+        lax.fori_loop(0, ROWS, update_halo, 0)
 
     for one in sent:
         one.wait_send()
@@ -443,16 +469,17 @@
             pltpu.VMEM((PARTS, SUB, TILES * BS), jnp.bfloat16),
             pltpu.VMEM((ROWS, BS, 3 * size), jnp.bfloat16),
             pltpu.VMEM((ITERS, 3 * size, BS), jnp.bfloat16),
+            pltpu.VMEM((ITERS - 1, 3 * size, BS), jnp.bfloat16),
             pltpu.VMEM((size, BS), f32),
-            pltpu.VMEM((ROWS, BS), f32),
-            pltpu.VMEM((size, BS), f32),
+            pltpu.VMEM((3, ROWS, BS), f32),
+            pltpu.VMEM((3 * size, BS), f32),
             pltpu.VMEM((2 * ITERS, 8, BS), f32),
             pltpu.VMEM((2 * ITERS * (RING - 1), 8, BS), f32),
             pltpu.SemaphoreType.DMA((5,)),
             pltpu.SemaphoreType.DMA((kinds,)),
             pltpu.SemaphoreType.DMA((kinds,)),
-            pltpu.SemaphoreType.DMA((2 * ITERS * PIECES,)),
-            pltpu.SemaphoreType.DMA((2 * ITERS * PIECES,)),
+            pltpu.SemaphoreType.DMA((2 * ITERS * PIECES + 2,)),
+            pltpu.SemaphoreType.DMA((2 * ITERS * PIECES + 2,)),
             pltpu.SemaphoreType.DMA((2 * ITERS * (RING - 1),)),
             pltpu.SemaphoreType.DMA((2 * ITERS * (RING - 1),)),
         ],

time: 86 us -> 81.2 us (0.944)
  Pallas kernels: 84.1 us -> 79.3 us
    pallas_call x1, Pallas kernels: 84.1 us -> 79.3 us  [local(): pl.pallas_call(kernel, out_shape=[field] * 5 + [jax.ShapeDtypeStruct((8,...]
where the time goes in v4:
time: 81.2 us; the launch traced here: 81.1 us
  Pallas kernels  79.3 us (98%)
  other arithmetic  1.11 us (1%)
    pallas_call x1, Pallas kernels, local(): pl.pallas_call(kernel, out_shape=[field] * 5 + [jax.ShapeDtypeStruct((8,...  79.3 us

profile of v4, /device:TPU:6, one launch (start us, length us, event | category | flops | bytes accessed | tf_op | source)
XLA Modules:
  0.0 81.1 jit_solution(12774834408136531496)
XLA Ops:
  0.6 79.3 %shard_map.68 = (f32[1024,128]{1,0:T(8,128)S(1)}, f32[1024,128]{1,0:T(8,128)S(1)}, f32[1024,128]{1,0:T(8,128)S(1)}, f32[1024,128]{1,0:T(8,128)S(1)}, f32[1024,128]{1,0:T(8,128)S(1)}, /*index=5*/f32[8,128]{1,0:T(8,128)S(1)}) custom-call(s32[8,16]{1,0:T(8,128)} %col_ref.1, s32[8]{0:T(128)} %length_ref.1, f32[1024,128]{1,0:T(8,128)} %targets_ref.1, ...), custom_call_target="tpu_custom_call" | custom-call | tf_op jit(solution)/shard_map/pallas_call | solution.py:459
  79.9 1.1 %multiply_subtract_fusion = (f32[1024,128]{1,0:T(8,128)}, f32[1024,128]{1,0:T(8,128)}) fusion(f32[1024,128]{1,0:T(8,128)S(1)} %get-tuple-element.10, f32[1024,128]{1,0:T(8,128)S(1)} %get-tuple-element.12, f32[1024,128]{1,0:T(8,128)S(1)} %get-tuple-element.13, f32[128]{0:T(128)S(1)} %get-tuple-element.17, f32[128]{0:T(128)S(1)} %get-tuple-element.16, ...), kind=kLoop, calls=%fused_computation | loop fusion | flops 1048576 | bytes 3671040 | tf_op jit(solution)/shard_map/sub | solution.py:491
  (1 shorter events, 0.0 us)

commit v5 on v4

--- a/solution.py
+++ b/solution.py
@@ -225,6 +225,7 @@
             launch(halo(0, side, piece))
     for g in range(2, PAIRS):
         densify(g)
+        send_own(g)
         spread(g, 0, part)
 
     def spread_ridge(t, unused):
@@ -233,6 +234,9 @@
         return unused
 
     lax.fori_loop(ROWS, 2 * ROWS, spread_ridge, 0)
+    for t in range(0, ROWS, 2):
+        band[t + 1, :, lanes(t, 1)] = jnp.zeros((BS, BS), jnp.bfloat16)
+        band[t, :, lanes(t + BAND, 1)] = jnp.zeros((BS, BS), jnp.bfloat16)
 
     def tile(index):
         return tiles[:, :, lanes(index, 1)].reshape(BS, BS)
@@ -254,6 +258,12 @@
         return jnp.dot(
             band[t, :, t * BS : (t + BAND) * BS], vec[step, t * BS : (t + BAND) * BS, :],
             preferred_element_type=jnp.float32,
+        )
+
+    def pair_whole(step, t):
+        left = band[t : t + 2, :, t * BS : (t + BAND + 1) * BS].reshape(2 * BS, (BAND + 1) * BS)
+        return jnp.dot(
+            left, vec[step, t * BS : (t + BAND + 1) * BS, :], preferred_element_type=jnp.float32
         )
 
     def fold(values):
@@ -290,10 +300,8 @@
         return values
 
     from_left(0)
-    send_own(2)
     from_right(0)
     from_left(1)
-    send_own(3)
     from_right(1)
     from_sides(0, 0)
     from_sides(1, 0)
@@ -368,7 +376,9 @@
 
     def image(step, t):
         r = res_ref[rows(t), :]
-        part_b = 0.5 * whole(step, t)
+        if t % 2 == 0:
+            acc[t * BS : (t + 2) * BS, :] = 0.5 * pair_whole(step, t)
+        part_b = acc[rows(t), :]
         wt = ridge[middle(t), :] * r + part_b
         w[rows(t), :] = wt
         if step < ITERS - 1:
@@ -391,7 +401,7 @@
                 sums[1] = sums[1] + fold(r * wt)
                 sums[2] = sums[2] + fold(r * q[rows(t), :] + d[rows(t), :] * wt)
             start_sum(step, 0, stack(sums))
-            early = 2 if step < ITERS - 1 else 0
+            early = 1 if step < ITERS - 1 else 0
             for piece in range(early):
                 start_halo(step + 1, piece)
             start_sum(step, 1, end_sum(step, 0))

time: 81.2 us -> 80.9 us (level)
  no operation moved by 1% of the time
where the time goes in v5:
time: 80.9 us; the launch traced here: 80.7 us
  Pallas kernels  79 us (98%)
  other arithmetic  1.11 us (1%)
    pallas_call x1, Pallas kernels, local(): pl.pallas_call(kernel, out_shape=[field] * 5 + [jax.ShapeDtypeStruct((8,...  79 us

profile of v5, /device:TPU:6, one launch (start us, length us, event | category | flops | bytes accessed | tf_op | source)
XLA Modules:
  0.0 80.7 jit_solution(15951012118678446774)
XLA Ops:
  0.6 79.0 %shard_map.68 = (f32[1024,128]{1,0:T(8,128)S(1)}, f32[1024,128]{1,0:T(8,128)S(1)}, f32[1024,128]{1,0:T(8,128)S(1)}, f32[1024,128]{1,0:T(8,128)S(1)}, f32[1024,128]{1,0:T(8,128)S(1)}, /*index=5*/f32[8,128]{1,0:T(8,128)S(1)}) custom-call(s32[8,16]{1,0:T(8,128)} %col_ref.1, s32[8]{0:T(128)} %length_ref.1, f32[1024,128]{1,0:T(8,128)} %targets_ref.1, ...), custom_call_target="tpu_custom_call" | custom-call | tf_op jit(solution)/shard_map/pallas_call | solution.py:469
  79.6 1.1 %multiply_subtract_fusion = (f32[1024,128]{1,0:T(8,128)}, f32[1024,128]{1,0:T(8,128)}) fusion(f32[1024,128]{1,0:T(8,128)S(1)} %get-tuple-element.10, f32[1024,128]{1,0:T(8,128)S(1)} %get-tuple-element.12, f32[1024,128]{1,0:T(8,128)S(1)} %get-tuple-element.13, f32[128]{0:T(128)S(1)} %get-tuple-element.17, f32[128]{0:T(128)S(1)} %get-tuple-element.16, ...), kind=kLoop, calls=%fused_computation | loop fusion | flops 1048576 | bytes 3671040 | tf_op jit(solution)/shard_map/sub | solution.py:501
  (1 shorter events, 0.0 us)
